TPU v7x, 32 devices: a whole 2x2x4 slice. The times are simulated.
32 devices in a mesh: groups: 1, expert: 8 (over z, core), dp: 4 (over y, x).
Axes of the slice: x: 2, y: 2, z: 4, core: 2. Of those that a mesh axis runs over, the one named last changes fastest.
Arguments:
- tokens: bfloat16 [128, 4096], P(('groups', 'expert', 'dp')), may hold values from -6 to 6
- expert_ids: int32 [128, 2], P(('groups', 'expert', 'dp')), may hold values from 0 to 7, as said below
- gate_weights: bfloat16 [128, 2], P(('groups', 'expert', 'dp')), may hold values from 0.099609375 to 1
- placement: int32 [2, 2], P('groups'), may hold values from 0 to 7, as said below
- w_gate: bfloat16 [8, 1536, 4096], P('expert', 'dp'), may hold values from -0.09375 to 0.09375
- w_up: bfloat16 [8, 1536, 4096], P('expert', 'dp'), may hold values from -0.09375 to 0.09375
- w_down: bfloat16 [8, 1536, 4096], P('expert', 'dp'), may hold values from -0.15625 to 0.15625
Outputs:
- mixed: bfloat16 [128, 4096], P(('groups', 'expert', 'dp'))
Inputs may be any that keep to these rules, and one draw needn't show every extreme that they name: `expert_ids`: each row names 2 different experts. In each aligned block of 16 rows (the tokens of one index of expert) no expert is named by more than 6 rows, and some expert is named by exactly that many. `placement`: row 0 holds 2 different experts; row 1 holds 2 different expert indices, none of which appears in row 0.
All inputs are finite; a program needn't handle non-finite values.
Results may differ from a plain program's by a relative error of at most 0.015.
Values may be sent and summed in bfloat16 or wider, within the bound.
A program may use at most 64 MiB of HBM per device.

v0:
```python
import jax
import jax.numpy as jnp
from jax import lax
from jax.sharding import PartitionSpec as P


def expert_block(rows, gate_w, up_w, down_w):
    contract = (((1,), (1,)), ((), ()))
    gate = lax.dot_general(rows, gate_w, contract, preferred_element_type=jnp.float32)
    up = lax.dot_general(rows, up_w, contract, preferred_element_type=jnp.float32)
    hidden = (jax.nn.silu(gate) * up).astype(jnp.bfloat16)
    return jnp.dot(hidden, down_w, preferred_element_type=jnp.float32).astype(jnp.bfloat16)


def body(tokens, expert_ids, gate_weights, placement, w_gate, w_up, w_down):
    group_source, group_gates = (
        lax.all_gather(tokens, "dp", axis=0, tiled=True),
        lax.all_gather(gate_weights, "dp", axis=0, tiled=True),
    )
    group_ids = lax.all_gather(expert_ids, "dp", axis=0, tiled=True)
    experts = lax.axis_size("expert")
    my_index = lax.axis_index("expert")
    width = tokens.shape[1]
    group = group_ids.shape[0]
    topk = expert_ids.shape[1]
    first = max(2, group * topk // experts)
    second = max(1, first // 2)
    slots = first + second
    pair_ids = group_ids.reshape(-1)
    onehot = (pair_ids[:, None] == jnp.arange(experts, dtype=jnp.int32)[None, :]).astype(jnp.int32)
    rank = jnp.sum((jnp.cumsum(onehot, axis=0) - onehot) * onehot, axis=1)
    match = pair_ids[:, None] == placement[0][None, :]
    listed = jnp.any(match, axis=1)
    keep = (rank < first) | listed & (rank < slots)
    dest = jnp.where(keep, pair_ids * slots + rank, -1)
    row_iota = jnp.arange(experts * slots, dtype=jnp.int32)
    pick = (dest[None, :] == row_iota[:, None]).reshape(experts * slots, group, topk)
    select = jnp.any(pick, axis=2).astype(jnp.bfloat16)
    weights_rows = jnp.sum(
        jnp.where(pick, group_gates[None, :, :].astype(jnp.float32), 0.0), axis=2
    ).astype(jnp.bfloat16)
    send = jnp.dot(select, group_source, preferred_element_type=jnp.float32).astype(jnp.bfloat16)
    received = lax.all_to_all(
        send.reshape(experts, slots, width), "expert", split_axis=0, concat_axis=0, tiled=True
    )
    main = expert_block(received[:, :first].reshape(-1, width), w_gate[0], w_up[0], w_down[0])
    active = jnp.any(placement[0] == my_index)
    extra_weights = (w_gate[0], w_up[0], w_down[0])
    extra_rows = received[:, first:].reshape(-1, width)
    extra = lax.cond(
        active,
        lambda: expert_block(extra_rows, extra_weights[0], extra_weights[1], extra_weights[2]),
        lambda: jnp.zeros((experts * second, width), jnp.bfloat16),
    )
    partial_value = jnp.concatenate(
        [main.reshape(experts, first, width), extra.reshape(experts, second, width)], axis=1
    )
    contract = (((0,), (0,)), ((), ()))
    summed = lax.psum_scatter(
        partial_value.astype(jnp.float32).astype(jnp.bfloat16),
        "dp",
        scatter_dimension=2,
        tiled=True,
    ).astype(jnp.float32)
    back = lax.all_to_all(
        summed.astype(jnp.bfloat16), "expert", split_axis=0, concat_axis=0, tiled=True
    ).astype(summed.dtype)
    group_cols = lax.dot_general(
        weights_rows.astype(jnp.float32),
        back.reshape(experts * slots, -1),
        contract,
        precision=lax.Precision.HIGHEST,
        preferred_element_type=jnp.float32,
    )
    mine_out = lax.all_to_all(
        group_cols.astype(jnp.bfloat16), "dp", split_axis=0, concat_axis=1, tiled=True
    ).astype(group_cols.dtype)
    return mine_out.astype(jnp.bfloat16)


def solution(mesh):
    placed = (
        P(("groups", "expert", "dp"), None),
        P(("groups", "expert", "dp"), None),
        P(("groups", "expert", "dp"), None),
        P("groups", None),
        P("expert", "dp", None),
        P("expert", "dp", None),
        P("expert", "dp", None),
    )
    return jax.shard_map(
        body,
        mesh=mesh,
        in_specs=placed,
        out_specs=P(("groups", "expert", "dp"), None),
        check_vma=False,
    )
```

profile of v0, /device:TPU:0, one launch (start us, length us, event | category | flops | bytes accessed | tf_op | source)
XLA Modules:
  0.0 121.7 jit_solution(14547632915415462673)
XLA Ops:
  6.5 0.0 copy-start
  6.5 9.9 %all-gather = s32[4,4,2]{1,2,0:T(2,128)S(1)} all-gather(s32[1,4,2]{1,2,0:T(2,128)} %bitcast.40), channel_id=1, replica_groups=mesh['groups'=1,'expert'=8,'dp'=4] {'dp'}, dimensions={0}, use_global_device_ids=true | all-gather | bytes 160 | tf_op jit(solution)/shard_map/all_gather | solution.py:20
  16.5 0.1 copy.32
  16.6 0.1 copy.38
  16.7 0.1 eq.50
  16.8 0.1 fusion.16
  16.9 0.1 reduce_window_sum.11
  16.9 0.2 select_reduce_fusion.1
  17.1 0.1 reduce_sum.21
  17.2 0.7 slice_bitcast_fusion
  17.9 0.1 compare_reduce_fusion.1
  18.0 0.1 reduce_or.30
  18.1 0.1 copy.35
  18.2 0.1 fusion.15
  18.3 8.3 %all-gather.2 = bf16[4,4,4096]{2,1,0:T(4,128)(2,1)S(1)} all-gather(bf16[1,4,4096]{2,1,0:T(4,128)(2,1)} %bitcast.38), channel_id=1, replica_groups=mesh['groups'=1,'expert'=8,'dp'=4] {'dp'}, dimensions={0}, use_global_device_ids=true | all-gather | bytes 163840 | tf_op jit(solution)/shard_map/all_gather | solution.py:17
  26.6 0.7 reshape.64
  27.2 1.2 convolution_convert_fusion.1
  28.5 0.9 reshape.55
  29.4 4.9 %all-to-all-start = ((bf16[8,6,4096]{2,1,0:T(8,128)(2,1)}), bf16[8,6,4096]{2,1,0:T(8,128)(2,1)}, u32[]{:S(2)}, u32[]{:S(2)}) async-start(bf16[8,6,4096]{2,1,0:T(8,128)(2,1)} %reshape.55), calls=%async_computation | async-start | bytes 1048576 | tf_op jit(solution)/shard_map/all_to_all | solution.py:43
  34.3 0.0 reduce-scatter.2.cloned.1.call-start
  34.3 1.3 %compare_reduce_fusion = pred[]{:T(512)} fusion(s32[]{:T(128)S(6)} %axis_index.15, s32[2,2]{1,0:T(2,128)} %param.12), kind=kLoop, calls=%fused_computation.32 | loop fusion | flops 3 | bytes 13 | tf_op jit(solution)/shard_map/reduce_or | solution.py:47
  36.3 13.4 %all-to-all-done = bf16[8,6,4096]{2,1,0:T(8,128)(2,1)} async-done(((bf16[8,6,4096]{2,1,0:T(8,128)(2,1)}), bf16[8,6,4096]{2,1,0:T(8,128)(2,1)}, u32[]{:S(2)}, u32[]{:S(2)}) %all-to-all-start) | async-done | bytes 393248 | tf_op jit(solution)/shard_map/all_to_all | solution.py:43
  49.7 1.8 %slice.13 = bf16[8,4,4096]{2,1,0:T(4,128)(2,1)} slice(bf16[8,6,4096]{2,1,0:T(8,128)(2,1)} %all-to-all-done), slice={[0:8], [0:4], [0:4096]} | slice | bytes 524288 | tf_op jit(solution)/shard_map/slice | solution.py:46
  51.5 1.0 reshape.56
  52.6 0.0 copy-done
  52.6 1.0 fusion.21
  53.6 5.6 %convolution_convert_fusion.2 = bf16[32,4096]{1,0:T(8,128)(2,1)} fusion(bf16[32,4096]{1,0:T(8,128)(2,1)S(1)} %reshape.56, f32[32,384]{1,0:T(8,128)S(1)} %fusion.21, bf16[1,384,4096]{2,1,0:T(8,128)(2,1)} %param.15, bf16[1,384,4096]{2,1,0:T(8,128)(2,1)} %param.14), kind=kOutput, calls=%fused_computation.11 | convolution fusion | flops 201531392 | bytes 6864896 | tf_op jit(solution)/shard_map/dot_general | solution.py:12
  59.2 1.1 reshape.57
  60.2 0.0 copy-start.1
  60.3 0.7 conditional.1
  60.3 0.7 reshape.48
  61.0 1.9 %pad_maximum_fusion = bf16[8,6,4096]{2,1,0:T(8,128)(2,1)} fusion(bf16[8,2,4096]{2,1,0:T(2,128)(2,1)} %get-tuple-element.23, bf16[8,4,4096]{2,1,0:T(4,128)(2,1)S(1)} %reshape.57), kind=kLoop, calls=%fused_computation.15 | loop fusion | flops 786432 | bytes 786432 | tf_op jit(solution)/shard_map/concatenate | solution.py:55
  62.9 0.0 reduce-scatter.2.cloned.1.call-update
  63.0 0.0 copy-done.1
  63.0 7.2 %all-gather.1 = bf16[4,4,2]{1,2,0:T(2,128)(2,1)S(1)} all-gather(bf16[1,4,2]{1,2,0:T(2,128)(2,1)S(1)} %bitcast.41), channel_id=1, replica_groups=mesh['groups'=1,'expert'=8,'dp'=4] {'dp'}, dimensions={0}, use_global_device_ids=true | all-gather | bytes 80 | tf_op jit(solution)/shard_map/all_gather | solution.py:18
  70.2 25.2 %reduce-scatter.2.cloned.1.call-done = bf16[8,6,1024]{2,1,0:T(8,128)(2,1)} async-done(((bf16[8,6,4096]{2,1,0:T(8,128)(2,1)}), bf16[8,6,1024]{2,1,0:T(8,128)(2,1)}) %reduce-scatter.2.cloned.1.call-update) | async-done | bytes 98320 | tf_op jit(solution)/shard_map/reduce_scatter | solution.py:59
  95.4 4.6 %all-to-all-start.1 = ((bf16[8,6,1024]{2,1,0:T(8,128)(2,1)}), bf16[8,6,1024]{2,1,0:T(8,128)(2,1)S(1)}, u32[]{:S(2)}, u32[]{:S(2)}) async-start(bf16[8,6,1024]{2,1,0:T(8,128)(2,1)} %reduce-scatter.2.cloned.1.call-done), calls=%async_computation.2 | async-start | bytes 262144 | tf_op jit(solution)/shard_map/all_to_all | solution.py:65
  100.0 0.1 reshape.65
  100.1 0.1 select_reduce_fusion
  100.2 6.6 %all-to-all-done.1 = bf16[8,6,1024]{2,1,0:T(8,128)(2,1)S(1)} async-done(((bf16[8,6,1024]{2,1,0:T(8,128)(2,1)}), bf16[8,6,1024]{2,1,0:T(8,128)(2,1)S(1)}, u32[]{:S(2)}, u32[]{:S(2)}) %all-to-all-start.1) | async-done | bytes 98336 | tf_op jit(solution)/shard_map/all_to_all | solution.py:65
  106.8 0.1 convolution_convert_fusion.3
  106.9 7.3 %all_to_all.29 = bf16[4,4,1024]{2,1,0:T(4,128)(2,1)S(1)} all-to-all(bf16[4,4,1024]{2,1,0:T(4,128)(2,1)S(1)} %all_to_all.22), channel_id=1, replica_groups=mesh['groups'=1,'expert'=8,'dp'=4] {'dp'}, dimensions={0} | all-to-all | bytes 65536 | tf_op jit(solution)/shard_map/all_to_all | solution.py:75
  114.2 0.6 copy.44
  (5 shorter events, 0.1 us)
Async XLA Ops:
  6.5 46.0 %copy-start = (bf16[1,384,4096]{2,1,0:T(8,128)(2,1)S(1)}, bf16[1,384,4096]{2,1,0:T(8,128)(2,1)}, u32[]{:S(2)}) copy-start(bf16[1,384,4096]{2,1,0:T(8,128)(2,1)} %param.13) | copy-start | bytes 9437188
  29.4 20.3 %all-to-all-start = ((bf16[8,6,4096]{2,1,0:T(8,128)(2,1)}), bf16[8,6,4096]{2,1,0:T(8,128)(2,1)}, u32[]{:S(2)}, u32[]{:S(2)}) async-start(bf16[8,6,4096]{2,1,0:T(8,128)(2,1)} %reshape.55), calls=%async_computation | async-start | bytes 1048576 | tf_op jit(solution)/shard_map/all_to_all | solution.py:43
  34.3 61.1 %reduce-scatter.2.cloned.1.call-start = ((), (), s32[]{:S(2)}) async-start(), calls=%async_computation.4 | async-start | bytes 655360 | tf_op jit(solution)/shard_map/reduce_scatter | solution.py:59
  60.2 2.7 %copy-start.1 = (bf16[4,2]{0,1:T(2,128)(2,1)S(1)}, bf16[4,2]{0,1:T(2,128)(2,1)}, u32[]{:S(2)}) copy-start(bf16[4,2]{0,1:T(2,128)(2,1)} %param.11) | copy-start | bytes 52
  95.4 11.4 %all-to-all-start.1 = ((bf16[8,6,1024]{2,1,0:T(8,128)(2,1)}), bf16[8,6,1024]{2,1,0:T(8,128)(2,1)S(1)}, u32[]{:S(2)}, u32[]{:S(2)}) async-start(bf16[8,6,1024]{2,1,0:T(8,128)(2,1)} %reduce-scatter.2.cloned.1.call-done), calls=%async_computation.2 | async-start | bytes 262144 | tf_op jit(solution)/shard_map/all_to_all | solution.py:65
Sparse Core Ops, SparseCore 0:
  63.1 32.2 reduce-scatter.1
where the time goes:
time: 122 us
  waiting for transfers between devices  45.2 us (37%)
  blocking collectives  32.7 us (27%)
  between operations  14.1 us (12%)
  starting transfers between devices  9.54 us (8%)
  local copies, waits for them, and re-layouts  8.28 us (7%)
  matrix products  7.95 us (7%)
  other arithmetic  3.84 us (3%)
    reduce_scatter x1, waiting for transfers between devices, body(): lax.psum_scatter(partial_value.astype(jnp.float32).astype(jnp.bfloat16),...  25.2 us
    all_to_all x1, waiting for transfers between devices, body(): lax.all_to_all(send.reshape(experts, slots, width), 'expert', split_axis=...  13.4 us
    all_gather x1, blocking collectives, body(): group_ids = lax.all_gather(expert_ids, 'dp', axis=0, tiled=True)  9.95 us
    all_gather x1, blocking collectives, body(): lax.all_gather(tokens, 'dp', axis=0, tiled=True)  8.3 us
    all_to_all x1, blocking collectives, body(): lax.all_to_all(group_cols.astype(jnp.bfloat16), 'dp', split_axis=0, conca...  7.29 us
    all_gather x1, blocking collectives, body(): lax.all_gather(gate_weights, 'dp', axis=0, tiled=True)  7.17 us
    all_to_all x1, waiting for transfers between devices, body(): lax.all_to_all(summed.astype(jnp.bfloat16), 'expert', split_axis=0, conca...  6.58 us
    dot_general x1, matrix products, expert_block(): jnp.dot(hidden, down_w, preferred_element_type=jnp.float32)  5.59 us
  transfers between devices with their start and end apart: 3, of which 3 were waited for; matrix products, arithmetic and copies ran while one was open for 1% of the time, Pallas kernels for 0%

commit v1 on v0

--- a/solution.py
+++ b/solution.py
@@ -2,6 +2,31 @@
 import jax.numpy as jnp
 from jax import lax
 from jax.sharding import PartitionSpec as P
+
+
+def split_up(x, dim, devices):
+    dims = x.shape
+    blocks = x.reshape(*dims[:dim], devices, dims[dim] // devices, *dims[dim + 1 :])
+    return jnp.moveaxis(blocks, dim, 0)
+
+
+def laid_out(tiles, dim):
+    shape = list(tiles.shape[1:])
+    shape[dim] *= tiles.shape[0]
+    return jnp.moveaxis(tiles, 0, dim).reshape(shape)
+
+
+def rotated_exchange(shard, axis, split_dim, concat_dim):
+    devices, index = (lax.axis_size(axis), lax.axis_index(axis))
+    pieces = split_up(shard, split_dim, devices)
+    finished = [pieces[index]]
+    for step in range(1, devices):
+        sent = pieces[(index + step) % devices]
+        finished.append(
+            lax.ppermute(sent, axis, [(i, (i + step) % devices) for i in range(devices)])
+        )
+    pieces = jnp.stack(finished)[(index - jnp.arange(devices)) % devices]
+    return laid_out(pieces, concat_dim)
 
 
 def expert_block(rows, gate_w, up_w, down_w):
@@ -72,9 +97,9 @@
         precision=lax.Precision.HIGHEST,
         preferred_element_type=jnp.float32,
     )
-    mine_out = lax.all_to_all(
-        group_cols.astype(jnp.bfloat16), "dp", split_axis=0, concat_axis=1, tiled=True
-    ).astype(group_cols.dtype)
+    mine_out = rotated_exchange(group_cols.astype(jnp.bfloat16), "dp", 0, 1).astype(
+        group_cols.dtype
+    )
     return mine_out.astype(jnp.bfloat16)
 
 

time: 122 us -> 123 us (level)
  blocking collectives: 32.7 us -> 25.4 us
  waiting for transfers between devices: 45.2 us -> 49.2 us
  starting transfers between devices: 9.54 us -> 13.1 us
    all_to_all x1 -> x0, blocking collectives: 7.29 us -> none  [body(): lax.all_to_all(group_cols.astype(jnp.bfloat16), 'dp', split_axis=0, conca...]
    ppermute x0 -> x3, waiting for transfers between devices: none -> 3.98 us  [rotated_exchange(): lax.ppermute(sent, axis, [(i, (i + step) % devices) for i in range(device...]
    ppermute x0 -> x3, starting transfers between devices: none -> 3.54 us  [rotated_exchange(): lax.ppermute(sent, axis, [(i, (i + step) % devices) for i in range(device...]
  transfers between devices with their start and end apart: 3 -> 6, of which waited for: 3 -> 6; matrix products, arithmetic and copies ran while one was open for 1% -> 1% of each run, Pallas kernels for 0% -> 0%
where the time goes in v1:
time: 123 us
  waiting for transfers between devices  49.2 us (40%)
  blocking collectives  25.4 us (21%)
  between operations  14.2 us (12%)
  starting transfers between devices  13.1 us (11%)
  local copies, waits for them, and re-layouts  8.88 us (7%)
  matrix products  7.95 us (6%)
  other arithmetic  3.89 us (3%)
    reduce_scatter x1, waiting for transfers between devices, body(): lax.psum_scatter(partial_value.astype(jnp.float32).astype(jnp.bfloat16),...  25.1 us
    all_to_all x1, waiting for transfers between devices, body(): lax.all_to_all(send.reshape(experts, slots, width), 'expert', split_axis=...  13.4 us
    all_gather x1, blocking collectives, body(): group_ids = lax.all_gather(expert_ids, 'dp', axis=0, tiled=True)  9.95 us
    all_gather x1, blocking collectives, body(): lax.all_gather(tokens, 'dp', axis=0, tiled=True)  8.3 us
    all_gather x1, blocking collectives, body(): lax.all_gather(gate_weights, 'dp', axis=0, tiled=True)  7.17 us
    all_to_all x1, waiting for transfers between devices, body(): lax.all_to_all(summed.astype(jnp.bfloat16), 'expert', split_axis=0, conca...  6.66 us
    dot_general x1, matrix products, expert_block(): jnp.dot(hidden, down_w, preferred_element_type=jnp.float32)  5.59 us
    all_to_all x1, starting transfers between devices, body(): lax.all_to_all(send.reshape(experts, slots, width), 'expert', split_axis=...  4.88 us
  transfers between devices with their start and end apart: 6, of which 6 were waited for; matrix products, arithmetic and copies ran while one was open for 1% of the time, Pallas kernels for 0%

profile of v1, /device:TPU:0, one launch (start us, length us, event | category | flops | bytes accessed | tf_op | source)
XLA Modules:
  0.0 122.6 jit_solution(4002861759043062737)
XLA Ops:
  6.5 0.0 copy-start
  6.5 9.9 %all-gather = s32[4,4,2]{1,2,0:T(2,128)S(1)} all-gather(s32[1,4,2]{1,2,0:T(2,128)} %bitcast.53), channel_id=1, replica_groups=mesh['groups'=1,'expert'=8,'dp'=4] {'dp'}, dimensions={0}, use_global_device_ids=true | all-gather | bytes 160 | tf_op jit(solution)/shard_map/all_gather | solution.py:45
  16.5 0.1 copy.32
  16.6 0.1 copy.38
  16.7 0.1 eq.56
  16.8 0.1 fusion.16
  16.9 0.1 reduce_window_sum.11
  16.9 0.2 select_reduce_fusion.1
  17.1 0.1 reduce_sum.21
  17.2 0.7 slice_bitcast_fusion
  17.9 0.1 compare_reduce_fusion.1
  18.0 0.1 reduce_or.30
  18.1 0.1 copy.35
  18.2 0.1 fusion.15
  18.3 8.3 %all-gather.2 = bf16[4,4,4096]{2,1,0:T(4,128)(2,1)S(1)} all-gather(bf16[1,4,4096]{2,1,0:T(4,128)(2,1)} %bitcast.48), channel_id=1, replica_groups=mesh['groups'=1,'expert'=8,'dp'=4] {'dp'}, dimensions={0}, use_global_device_ids=true | all-gather | bytes 163840 | tf_op jit(solution)/shard_map/all_gather | solution.py:42
  26.6 0.7 reshape.126
  27.2 1.2 convolution_convert_fusion.1
  28.5 0.9 reshape.107
  29.4 4.9 %all-to-all-start = ((bf16[8,6,4096]{2,1,0:T(8,128)(2,1)}), bf16[8,6,4096]{2,1,0:T(8,128)(2,1)}, u32[]{:S(2)}, u32[]{:S(2)}) async-start(bf16[8,6,4096]{2,1,0:T(8,128)(2,1)} %reshape.107), calls=%async_computation | async-start | bytes 1048576 | tf_op jit(solution)/shard_map/all_to_all | solution.py:68
  34.3 0.0 reduce-scatter.2.cloned.1.call-start
  34.3 1.3 %compare_reduce_fusion = pred[]{:T(512)} fusion(s32[]{:T(128)S(6)} %axis_index.23, s32[2,2]{1,0:T(2,128)} %param.12), kind=kLoop, calls=%fused_computation.42 | loop fusion | flops 3 | bytes 13 | tf_op jit(solution)/shard_map/reduce_or | solution.py:72
  36.3 13.4 %all-to-all-done = bf16[8,6,4096]{2,1,0:T(8,128)(2,1)} async-done(((bf16[8,6,4096]{2,1,0:T(8,128)(2,1)}), bf16[8,6,4096]{2,1,0:T(8,128)(2,1)}, u32[]{:S(2)}, u32[]{:S(2)}) %all-to-all-start) | async-done | bytes 393248 | tf_op jit(solution)/shard_map/all_to_all | solution.py:68
  49.7 1.8 %slice.15 = bf16[8,4,4096]{2,1,0:T(4,128)(2,1)} slice(bf16[8,6,4096]{2,1,0:T(8,128)(2,1)} %all-to-all-done), slice={[0:8], [0:4], [0:4096]} | slice | bytes 524288 | tf_op jit(solution)/shard_map/slice | solution.py:71
  51.5 1.0 reshape.108
  52.6 0.0 copy-done
  52.6 1.0 fusion.23
  53.6 5.6 %convolution_convert_fusion.2 = bf16[32,4096]{1,0:T(8,128)(2,1)} fusion(bf16[32,4096]{1,0:T(8,128)(2,1)S(1)} %reshape.108, f32[32,384]{1,0:T(8,128)S(1)} %fusion.23, bf16[1,384,4096]{2,1,0:T(8,128)(2,1)} %param.15, bf16[1,384,4096]{2,1,0:T(8,128)(2,1)} %param.14), kind=kOutput, calls=%fused_computation.12 | convolution fusion | flops 201531392 | bytes 6864896 | tf_op jit(solution)/shard_map/dot_general | solution.py:37
  59.2 1.1 reshape.109
  60.2 0.0 copy-start.1
  60.3 0.7 conditional.1
  60.3 0.7 reshape.98
  61.0 1.9 %pad_maximum_fusion = bf16[8,6,4096]{2,1,0:T(8,128)(2,1)} fusion(bf16[8,2,4096]{2,1,0:T(2,128)(2,1)} %get-tuple-element.27, bf16[8,4,4096]{2,1,0:T(4,128)(2,1)S(1)} %reshape.109), kind=kLoop, calls=%fused_computation.16 | loop fusion | flops 786432 | bytes 786432 | tf_op jit(solution)/shard_map/concatenate | solution.py:80
  62.9 0.0 reduce-scatter.2.cloned.1.call-update
  63.0 0.0 copy-done.1
  63.0 7.2 %all-gather.1 = bf16[4,4,2]{1,2,0:T(2,128)(2,1)S(1)} all-gather(bf16[1,4,2]{1,2,0:T(2,128)(2,1)S(1)} %bitcast.54), channel_id=1, replica_groups=mesh['groups'=1,'expert'=8,'dp'=4] {'dp'}, dimensions={0}, use_global_device_ids=true | all-gather | bytes 80 | tf_op jit(solution)/shard_map/all_gather | solution.py:43
  70.2 0.1 reshape.127
  70.2 25.1 %reduce-scatter.2.cloned.1.call-done = bf16[8,6,1024]{2,1,0:T(8,128)(2,1)} async-done(((bf16[8,6,4096]{2,1,0:T(8,128)(2,1)}), bf16[8,6,1024]{2,1,0:T(8,128)(2,1)}) %reduce-scatter.2.cloned.1.call-update) | async-done | bytes 98320 | tf_op jit(solution)/shard_map/reduce_scatter | solution.py:84
  95.4 4.6 %all-to-all-start.1 = ((bf16[8,6,1024]{2,1,0:T(8,128)(2,1)}), bf16[8,6,1024]{2,1,0:T(8,128)(2,1)S(1)}, u32[]{:S(2)}, u32[]{:S(2)}) async-start(bf16[8,6,1024]{2,1,0:T(8,128)(2,1)} %reduce-scatter.2.cloned.1.call-done), calls=%async_computation.2 | async-start | bytes 262144 | tf_op jit(solution)/shard_map/all_to_all | solution.py:90
  100.0 0.1 select_reduce_fusion
  100.1 6.7 %all-to-all-done.1 = bf16[8,6,1024]{2,1,0:T(8,128)(2,1)S(1)} async-done(((bf16[8,6,1024]{2,1,0:T(8,128)(2,1)}), bf16[8,6,1024]{2,1,0:T(8,128)(2,1)S(1)}, u32[]{:S(2)}, u32[]{:S(2)}) %all-to-all-start.1) | async-done | bytes 98336 | tf_op jit(solution)/shard_map/all_to_all | solution.py:90
  106.8 0.1 convolution_convert_fusion.3
  107.0 1.5 %collective-permute-start.2 = (bf16[4,1024]{1,0:T(4,128)(2,1)S(1)}, bf16[4,1024]{1,0:T(4,128)(2,1)S(1)}, u32[]{:S(2)}, u32[]{:S(2)}) collective-permute-start(bf16[4,1024]{1,0:T(4,128)(2,1)S(1)} %get-tuple-element.24), channel_id=1, source_target_pairs={{0,3},{1,0},{2,1},{3,2},{4,7},{5,4},{6,5},{7,6},{8,11},{9,8},{10,9... | collective-permute-start | bytes 24584 | tf_op jit(solution)/shard_map/ppermute | solution.py:26
  108.5 1.5 %collective-permute-start.1 = (bf16[4,1024]{1,0:T(4,128)(2,1)S(1)}, bf16[4,1024]{1,0:T(4,128)(2,1)S(1)}, u32[]{:S(2)}, u32[]{:S(2)}) collective-permute-start(bf16[4,1024]{1,0:T(4,128)(2,1)S(1)} %get-tuple-element.25), channel_id=1, source_target_pairs={{0,2},{1,3},{2,0},{3,1},{4,6},{5,7},{6,4},{7,5},{8,10},{9,11},{10,... | collective-permute-start | bytes 24584 | tf_op jit(solution)/shard_map/ppermute | solution.py:26
  110.0 0.6 collective-permute-start
  110.5 0.2 collective-permute-done.2
  110.7 1.5 %collective-permute-done.1 = bf16[4,1024]{1,0:T(4,128)(2,1)S(1)} collective-permute-done((bf16[4,1024]{1,0:T(4,128)(2,1)S(1)}, bf16[4,1024]{1,0:T(4,128)(2,1)S(1)}, u32[]{:S(2)}, u32[]{:S(2)}) %collective-permute-start.1) | collective-permute-done | bytes 8224 | tf_op jit(solution)/shard_map/ppermute | solution.py:26
  112.1 2.4 %collective-permute-done = bf16[4,1024]{1,0:T(4,128)(2,1)S(1)} collective-permute-done((bf16[4,1024]{1,0:T(4,128)(2,1)S(1)}, bf16[4,1024]{1,0:T(4,128)(2,1)S(1)}, u32[]{:S(2)}, u32[]{:S(2)}) %collective-permute-start) | collective-permute-done | bytes 8224 | tf_op jit(solution)/shard_map/ppermute | solution.py:26
  114.5 1.2 gather_fusion
  (9 shorter events, 0.2 us)
Async XLA Ops:
  6.5 46.0 %copy-start = (bf16[1,384,4096]{2,1,0:T(8,128)(2,1)S(1)}, bf16[1,384,4096]{2,1,0:T(8,128)(2,1)}, u32[]{:S(2)}) copy-start(bf16[1,384,4096]{2,1,0:T(8,128)(2,1)} %param.13) | copy-start | bytes 9437188
  29.4 20.3 %all-to-all-start = ((bf16[8,6,4096]{2,1,0:T(8,128)(2,1)}), bf16[8,6,4096]{2,1,0:T(8,128)(2,1)}, u32[]{:S(2)}, u32[]{:S(2)}) async-start(bf16[8,6,4096]{2,1,0:T(8,128)(2,1)} %reshape.107), calls=%async_computation | async-start | bytes 1048576 | tf_op jit(solution)/shard_map/all_to_all | solution.py:68
  34.3 61.1 %reduce-scatter.2.cloned.1.call-start = ((), (), s32[]{:S(2)}) async-start(), calls=%async_computation.3 | async-start | bytes 655360 | tf_op jit(solution)/shard_map/reduce_scatter | solution.py:84
  60.2 2.7 %copy-start.1 = (bf16[4,2]{0,1:T(2,128)(2,1)S(1)}, bf16[4,2]{0,1:T(2,128)(2,1)}, u32[]{:S(2)}) copy-start(bf16[4,2]{0,1:T(2,128)(2,1)} %param.11) | copy-start | bytes 52
  95.4 11.4 %all-to-all-start.1 = ((bf16[8,6,1024]{2,1,0:T(8,128)(2,1)}), bf16[8,6,1024]{2,1,0:T(8,128)(2,1)S(1)}, u32[]{:S(2)}, u32[]{:S(2)}) async-start(bf16[8,6,1024]{2,1,0:T(8,128)(2,1)} %reduce-scatter.2.cloned.1.call-done), calls=%async_computation.2 | async-start | bytes 262144 | tf_op jit(solution)/shard_map/all_to_all | solution.py:90
  107.0 3.7 %collective-permute-start.2 = (bf16[4,1024]{1,0:T(4,128)(2,1)S(1)}, bf16[4,1024]{1,0:T(4,128)(2,1)S(1)}, u32[]{:S(2)}, u32[]{:S(2)}) collective-permute-start(bf16[4,1024]{1,0:T(4,128)(2,1)S(1)} %get-tuple-element.24), channel_id=1, source_target_pairs={{0,3},{1,0},{2,1},{3,2},{4,7},{5,4},{6,5},{7,6},{8,11},{9,8},{10,9... | collective-permute-start | bytes 24584 | tf_op jit(solution)/shard_map/ppermute | solution.py:26
  108.5 3.7 %collective-permute-start.1 = (bf16[4,1024]{1,0:T(4,128)(2,1)S(1)}, bf16[4,1024]{1,0:T(4,128)(2,1)S(1)}, u32[]{:S(2)}, u32[]{:S(2)}) collective-permute-start(bf16[4,1024]{1,0:T(4,128)(2,1)S(1)} %get-tuple-element.25), channel_id=1, source_target_pairs={{0,2},{1,3},{2,0},{3,1},{4,6},{5,7},{6,4},{7,5},{8,10},{9,11},{10,... | collective-permute-start | bytes 24584 | tf_op jit(solution)/shard_map/ppermute | solution.py:26
  110.0 4.5 %collective-permute-start = (bf16[4,1024]{1,0:T(4,128)(2,1)S(1)}, bf16[4,1024]{1,0:T(4,128)(2,1)S(1)}, u32[]{:S(2)}, u32[]{:S(2)}) collective-permute-start(bf16[4,1024]{1,0:T(4,128)(2,1)S(1)} %get-tuple-element.26), channel_id=1, source_target_pairs={{0,1},{1,2},{2,3},{3,0},{4,5},{5,6},{6,7},{7,4},{8,9},{9,10},{10,1... | collective-permute-start | bytes 24584 | tf_op jit(solution)/shard_map/ppermute | solution.py:26
Sparse Core Ops, SparseCore 0:
  63.1 32.2 reduce-scatter.1
